TPU v7x, 32 devices: a whole 2x2x4 slice. The times are simulated.
32 devices in a mesh: hour: 2 (over y), pair: 4 (over z), freq: 2 (over x), sub: 2 (over core).
Axes of the slice: x: 2, y: 2, z: 4, core: 2. Of those that a mesh axis runs over, the one named last changes fastest.
Arguments:
- raw: float32 [512, 4096], P('freq', ('hour', 'pair', 'sub')), parts along dimension 1, may hold values from -60 to 60
- offsets: int32 [16], P(('hour', 'pair', 'sub')), parts along dimension 0, may hold values from 0 to 255
- pair_mask: int32 [4, 2], P('pair'), may hold values 0 or 1
Outputs:
- correlations: bfloat16 [8, 3, 128, 128, 256], P(('hour', 'pair'), None, 'sub', 'freq'), parts along dimension 0
There are 2 independent parts, one for each index of `hour`. A program takes and returns all parts, laid end to end along the dimension named above; an argument that names none is the same for every part. Nothing has to cross between parts.
All inputs are finite; a program needn't handle non-finite values. No bound on the sum of `pair_mask` on one device may be relied on, other than what follows from the above.
Results may differ from a plain program's by a relative error of at most 0.0056.
Values may be sent and summed in bfloat16 or wider, within the bound.
No kernel may reach another device: no remote copies, remote signals or barrier semaphores. Data moves between devices by JAX's collectives and lax.ppermute only.
A program may use at most 64 MiB of HBM per device.

v0:
```python
import math

import jax
import jax.numpy as jnp
from jax import lax
from jax.sharding import PartitionSpec as P

F = 256
REACH = 2
LAGS = 256
STEP = 256


def shifted(value, axis, steps):
    count = lax.axis_size(axis)
    initial, last = (max(0, -steps), min(count, count - steps))
    return lax.ppermute(value, axis, [(source, source + steps) for source in range(initial, last)])


def dft_basis(freqs, imaginary, span):
    samples = jnp.arange(span, dtype=jnp.int32)
    phase = samples[:, None] * freqs[None, :] % span
    angle = 2.0 * math.pi / span * phase.astype(jnp.float32)
    values = jnp.where(imaginary[None, :], -jnp.sin(angle), jnp.cos(angle)) / math.sqrt(span)
    return values.astype(jnp.bfloat16)


def lag_basis(freqs, imaginary, span, lag_count, bins):
    delays = jnp.arange(lag_count, dtype=jnp.int32) - lag_count // 2
    phase = freqs[:, None] * delays[None, :] % span
    angle = 2.0 * math.pi / span * phase.astype(jnp.float32)
    values = jnp.where(imaginary[:, None], -jnp.sin(angle), jnp.cos(angle)) / math.sqrt(bins)
    return values.astype(jnp.bfloat16)


def tapered(windows):
    span = windows.shape[-1]
    centred = windows - jnp.mean(windows, axis=-1, keepdims=True)
    power = jnp.mean(centred * centred, axis=-1, keepdims=True)
    ticks = jnp.arange(span, dtype=jnp.float32)
    hann_taper = 0.5 - 0.5 * jnp.cos(2.0 * math.pi / span * ticks)
    return (centred * lax.rsqrt(power + 1e-05) * hann_taper).astype(jnp.bfloat16)


def cross_spectra(left, right, factor):
    row_count = left.shape[0]
    col_count = right.shape[0]
    bins = left.shape[3]
    turned = jnp.stack([left[:, :, 1], -left[:, :, 0]], axis=2)
    real_part = jnp.einsum("rwtf,cwtf->rcf", left, right, preferred_element_type=jnp.float32)
    imaginary_part = jnp.einsum("rwtf,cwtf->rcf", turned, right, preferred_element_type=jnp.float32)
    joined = jnp.stack([real_part, imaginary_part], axis=2)
    return joined.reshape(row_count, col_count, 2 * bins) * factor


def body(raw, offsets, pair_mask):
    span = 2 * F
    freq_count = lax.axis_size("freq")
    segment = raw.shape[1]
    extra = (span + segment - 1) // segment
    pieces = [raw]
    for ahead in range(1, extra + 1):
        pieces.append(shifted(raw, ("pair", "sub"), -ahead))
    record = jnp.concatenate(pieces, axis=1)
    starts = jnp.arange(offsets.shape[0], dtype=jnp.int32) * STEP + offsets
    windows = jax.vmap(lambda begin: lax.dynamic_slice_in_dim(record, begin, span, 1), out_axes=1)(
        starts
    )
    column = jnp.arange(span, dtype=jnp.int32)
    freqs = column % F
    imaginary = column >= F
    basis = dft_basis(freqs, imaginary, span)
    spectra = jnp.dot(tapered(windows), basis, preferred_element_type=jnp.float32).astype(
        jnp.bfloat16
    )
    spectra = spectra.reshape(spectra.shape[0], spectra.shape[1], 2, F)
    halves = lax.all_to_all(
        lax.all_to_all(spectra, "freq", split_axis=3, concat_axis=0, tiled=True),
        ("pair", "sub"),
        split_axis=0,
        concat_axis=1,
        tiled=True,
    )
    block = lax.all_gather(halves, "sub", axis=0, tiled=True)
    factor = 1.0 / halves.shape[1]
    full_block = lax.all_gather(block, "freq", axis=3, tiled=True)
    row_count = halves.shape[0]
    rows = lax.dynamic_slice_in_dim(full_block, lax.axis_index("sub") * row_count, row_count, 0)
    col_count = full_block.shape[0] // freq_count
    own_columns = lax.dynamic_slice_in_dim(
        full_block, lax.axis_index("freq") * col_count, col_count, 0
    )
    lag_table = lag_basis(freqs, imaginary, span, LAGS, F)

    def transform(partner):
        term = cross_spectra(rows, partner, factor).astype(jnp.bfloat16)
        return jnp.einsum(
            "pcf,fl->pcl", term, lag_table, preferred_element_type=jnp.float32
        ).astype(jnp.bfloat16)

    def silent(unused):
        return jnp.zeros((row_count, col_count, LAGS), jnp.bfloat16)

    outputs = [transform(own_columns)]
    for offset in range(1, REACH + 1):
        partner = shifted(own_columns, "pair", -offset)
        outputs.append(lax.cond(pair_mask[0, offset - 1] == 1, transform, silent, partner))
    result = jnp.stack(outputs)
    return result[None]


def solution(mesh):
    return jax.shard_map(
        body,
        mesh=mesh,
        in_specs=(P("freq", ("hour", "pair", "sub")), P(("hour", "pair", "sub")), P("pair", None)),
        out_specs=P(("hour", "pair"), None, "sub", "freq", None),
        check_vma=False,
    )
```

profile of v0, /device:TPU:0, one launch (start us, length us, event | category | flops | bytes accessed | tf_op | source)
XLA Modules:
  0.0 169.6 jit_solution(11203225285981303011)
XLA Ops:
  6.5 0.0 copy-start.1
  6.5 0.0 all-gather.4.cloned.1.call-start
  6.5 1.4 collective-permute-start.1
  8.0 1.3 collective-permute-start
  10.0 8.1 %collective-permute-done.1 = f32[256,256]{1,0:T(8,128)S(1)} collective-permute-done((f32[256,256]{1,0:T(8,128)}, f32[256,256]{1,0:T(8,128)S(1)}, u32[]{:S(2)}, u32[]{:S(2)}) %collective-permute-start.1) | collective-permute-done | bytes 262176 | tf_op jit(solution)/shard_map/ppermute | solution.py:17
  18.1 0.0 collective-permute-done
  18.1 1.4 fusion.57
  19.5 0.2 fusion.30
  19.8 4.5 %convolution_convert_fusion = bf16[256,512]{1,0:T(8,128)(2,1)S(1)} fusion(s32[512]{0:T(512)S(1)} %add_select_fusion.2, pred[512]{0:T(512)(128)(4,1)S(1)} %iota_compare_fusion, f32[256,512]{1,0:T(8,128)S(1)} %get-tuple-element.49, f32[512]{0:T(512)S(1)} %multiply_subtract_fusion, f32[256]{0:T(256)S(1)} %add_rsqrt_fusion, f32[256]{0:T(256)S(1)} %broadcast_multiply_fusion), kind=kOutput, calls=%fused_computation.31 | convolution fusion | flops 139591680 | bytes 793088 | tf_op jit(solution)/shard_map/dot_general | solution.py:73
  24.3 0.1 reshape.146
  24.3 0.5 copy.29
  24.9 7.9 %all_to_all.36 = bf16[256,1,2,256]{0,2,1,3:T(2,128)(2,1)S(1)} all-to-all(bf16[256,1,2,256]{0,2,1,3:T(2,128)(2,1)S(1)} %copy.29), channel_id=1, replica_groups=mesh['hour'=2,'pair'=4,'freq'=2,'sub'=2] {'freq'}, dimensions={3} | all-to-all | bytes 524288 | tf_op jit(solution)/shard_map/all_to_all | solution.py:78
  32.8 0.2 copy.31
  33.0 0.3 copy.32
  33.2 15.3 %all_to_all.37 = bf16[512,1,2,128]{3,2,1,0:T(2,128)(2,1)S(1)} all-to-all(bf16[512,1,2,128]{3,2,1,0:T(2,128)(2,1)S(1)} %copy.32), channel_id=1, replica_groups=mesh['hour'=2,'pair'=4,'freq'=2,'sub'=2] {'pair','sub'}, dimensions={0} | all-to-all | bytes 524288 | tf_op jit(solution)/shard_map/all_to_all | solution.py:77
  48.5 2.3 %all-gather = bf16[128,8,1,2,128]{4,0,1,3,2:T(8,128)(2,1)} all-gather(bf16[64,8,1,2,128]{4,0,1,3,2:T(8,128)(2,1)S(1)} %bitcast.102), channel_id=2, replica_groups=mesh['hour'=2,'pair'=4,'freq'=2,'sub'=2] {'sub'}, dimensions={0}, use_global_device_ids=true | all-gather | bytes 786432 | tf_op jit(solution)/shard_map/all_gather | solution.py:84
  50.9 0.0 all-gather.4.cloned.1.call-update
  50.9 0.0 copy-done.1
  50.9 0.7 fusion.62
  52.9 2.6 %multiply_convert_fusion.2 = bf16[512,256]{1,0:T(8,128)(2,1)S(1)} fusion(s32[256]{0:T(256)S(1)} %iota_add_fusion, s32[512]{0:T(512)S(1)} %add_select_fusion.2, pred[512]{0:T(512)(128)(4,1)S(1)} %iota_compare_fusion), kind=kLoop, calls=%fused_computation.61 | loop fusion | flops 2359296 | bytes 265728 | tf_op jit(solution)/shard_map/convert_element_type | solution.py:33
  55.6 14.7 %all-gather.4.cloned.1.call-done = bf16[128,8,1,2,256]{4,0,1,3,2:T(8,128)(2,1)} async-done(((bf16[128,8,1,2,128]{4,0,1,3,2:T(8,128)(2,1)}), bf16[128,8,1,2,256]{4,0,1,3,2:T(8,128)(2,1)}) %all-gather.4.cloned.1.call-update) | async-done | bytes 1048592 | tf_op jit(solution)/shard_map/all_gather | solution.py:86
  70.3 1.3 constant_dynamic-slice_fusion
  71.6 1.1 copy.37
  72.7 1.3 collective-permute-start.3
  74.0 1.5 collective-permute-start.2
  75.4 1.0 copy.34
  76.4 1.0 copy.35
  77.4 0.1 fusion.61
  77.5 1.4 convolution_bitcast_fusion.5
  78.9 1.4 convolution_bitcast_fusion.4
  80.3 4.6 %fusion.12 = bf16[64,64,2,256]{0,1,3,2:T(8,128)(2,1)} fusion(f32[64,64,1,256]{0,1,3,2:T(8,128)S(1)} %convolution_bitcast_fusion.4, f32[64,64,1,256]{0,1,3,2:T(8,128)S(1)} %convolution_bitcast_fusion.5), kind=kLoop, calls=%fused_computation.23 | loop fusion | flops 6291456 | bytes 12582912 | tf_op jit(solution)/shard_map/convert_element_type | solution.py:96
  84.9 12.0 %copy.36 = bf16[64,64,512]{2,1,0:T(8,128)(2,1)} copy(bf16[64,64,512]{0,1,2:T(8,128)(2,1)} %bitcast.98) | data formatting | bytes 8388608 | tf_op jit(solution)/shard_map/convert_element_type | solution.py:96
  96.9 7.0 %convert_bitcast_fusion.2 = bf16[1,64,64,256]{3,2,1,0:T(8,128)(2,1)} fusion(bf16[64,64,512]{2,1,0:T(8,128)(2,1)} %copy.36, s32[256]{0:T(256)S(1)} %iota_add_fusion, s32[512]{0:T(512)S(1)} %add_select_fusion.2, pred[512]{0:T(512)(128)(4,1)S(1)} %iota_compare_fusion), kind=kOutput, calls=%fused_computation.27 | convolution fusion | flops 1077149696 | bytes 6295040 | tf_op jit(solution)/shard_map/pcf,fl->pcl/dot_general | solution.py:97
  103.8 0.0 collective-permute-done.3
  103.8 24.2 %conditional.3 = (bf16[1,64,64,256]{3,2,1,0:T(8,128)(2,1)S(1)}) conditional(s32[]{:T(128)} %bitcast.42, () %tuple.23, (bf16[64,8,2,256]{3,1,2,0:T(8,128)(2,1)S(1)}, bf16[64,8,2,256]{0,1,2,3:T(8,128)(2,1)S(1)}, bf16[512,256]{1,0:T(8,128)(2,1)S(1)}) %tuple.44), branch_computations={%region_4.5_spmd, %region_5.6_spmd} | conditional | flops 1148583936 | bytes 40108040 | solution.py:107
  103.8 1.3 copy.40
  105.1 0.1 fusion.60
  105.3 1.4 convolution_bitcast_fusion.2
  106.7 1.4 convolution_bitcast_fusion.3
  108.0 4.6 %fusion.6 = bf16[64,64,2,256]{0,1,3,2:T(8,128)(2,1)} fusion(f32[64,64,1,256]{0,1,3,2:T(8,128)S(1)} %convolution_bitcast_fusion.2, f32[64,64,1,256]{0,1,3,2:T(8,128)S(1)} %convolution_bitcast_fusion.3), kind=kLoop, calls=%fused_computation.12 | loop fusion | flops 6291456 | bytes 12582912 | tf_op jit(solution)/shard_map/cond/branch_1_fun/convert_element_type | solution.py:96
  112.7 12.0 %copy.28 = bf16[64,64,512]{2,1,0:T(8,128)(2,1)} copy(bf16[64,64,512]{0,1,2:T(8,128)(2,1)} %bitcast.99) | data formatting | bytes 8388608 | tf_op jit(solution)/shard_map/cond/branch_1_fun/convert_element_type | solution.py:96
  124.7 3.4 %convert_bitcast_fusion.1 = bf16[1,64,64,256]{3,2,1,0:T(8,128)(2,1)S(1)} fusion(bf16[64,64,512]{2,1,0:T(8,128)(2,1)} %copy.28, bf16[512,256]{1,0:T(8,128)(2,1)S(1)} %get-tuple-element.30), kind=kOutput, calls=%fused_computation.15 | convolution fusion | flops 1074790400 | bytes 6553600 | tf_op jit(solution)/shard_map/cond/branch_1_fun/pcf,fl->pcl/dot_general | solution.py:97
  128.1 0.0 copy-start
  128.1 0.0 collective-permute-done.2
  128.1 1.3 copy-done
  129.4 26.9 %conditional.2 = (bf16[1,64,64,256]{3,2,1,0:T(8,128)(2,1)}) conditional(s32[]{:T(128)} %bitcast.40, () %tuple.21, (bf16[64,8,2,256]{3,1,2,0:T(8,128)(2,1)}, bf16[64,8,2,256]{0,1,2,3:T(8,128)(2,1)S(1)}, bf16[512,256]{1,0:T(8,128)(2,1)S(1)}) %tuple.45), branch_computations={%region_2.3_spmd, %region_3.4_spmd} | conditional | flops 1148583936 | bytes 40108040 | solution.py:107
  129.4 2.6 %copy.38 = bf16[64,8,2,256]{0,1,2,3:T(8,128)(2,1)S(1)} copy(bf16[64,8,2,256]{3,1,2,0:T(8,128)(2,1)} %get-tuple-element.42) | data formatting | bytes 1048576 | tf_op jit(solution)/shard_map
  132.1 0.1 fusion.59
  132.2 1.4 convolution_bitcast_fusion
  133.6 1.4 convolution_bitcast_fusion.1
  135.0 4.6 %fusion = bf16[64,64,2,256]{0,1,3,2:T(8,128)(2,1)} fusion(f32[64,64,1,256]{0,1,3,2:T(8,128)S(1)} %convolution_bitcast_fusion, f32[64,64,1,256]{0,1,3,2:T(8,128)S(1)} %convolution_bitcast_fusion.1), kind=kLoop, calls=%fused_computation.1 | loop fusion | flops 6291456 | bytes 12582912 | tf_op jit(solution)/shard_map/cond/branch_1_fun/convert_element_type | solution.py:96
  139.6 12.0 %copy.26 = bf16[64,64,512]{2,1,0:T(8,128)(2,1)} copy(bf16[64,64,512]{0,1,2:T(8,128)(2,1)} %bitcast.100) | data formatting | bytes 8388608 | tf_op jit(solution)/shard_map/cond/branch_1_fun/convert_element_type | solution.py:96
  151.6 4.8 %convert_bitcast_fusion = bf16[1,64,64,256]{3,2,1,0:T(8,128)(2,1)} fusion(bf16[64,64,512]{2,1,0:T(8,128)(2,1)} %copy.26, bf16[512,256]{1,0:T(8,128)(2,1)S(1)} %get-tuple-element.27), kind=kOutput, calls=%fused_computation.4 | convolution fusion | flops 1074790400 | bytes 6553600 | tf_op jit(solution)/shard_map/cond/branch_1_fun/pcf,fl->pcl/dot_general | solution.py:97
  156.3 6.4 %maximum_bitcast_fusion = bf16[1,3,64,64,256]{4,3,2,1,0:T(8,128)(2,1)} fusion(bf16[1,64,64,256]{3,2,1,0:T(8,128)(2,1)} %copy-done, bf16[1,64,64,256]{3,2,1,0:T(8,128)(2,1)} %get-tuple-element.60, bf16[1,64,64,256]{3,2,1,0:T(8,128)(2,1)} %convert_bitcast_fusion.2), kind=kLoop, calls=%fused_computation.24 | loop fusion | flops 6291456 | bytes 12582912 | tf_op jit(solution)/shard_map/broadcast_in_dim | solution.py:109
  (8 shorter events, 0.1 us)
Async XLA Ops:
  6.5 44.3 %copy-start.1 = (s32[1,2]{1,0:T(1,128)S(1)}, s32[1,2]{1,0:T(1,128)}, u32[]{:S(2)}) copy-start(s32[1,2]{1,0:T(1,128)} %param.9) | copy-start | bytes 28
  6.5 63.7 %all-gather.4.cloned.1.call-start = ((), (), s32[]{:S(2)}) async-start(), calls=%async_computation.2 | async-start | bytes 1572864 | tf_op jit(solution)/shard_map/all_gather | solution.py:86
  6.5 11.6 %collective-permute-start.1 = (f32[256,256]{1,0:T(8,128)}, f32[256,256]{1,0:T(8,128)S(1)}, u32[]{:S(2)}, u32[]{:S(2)}) collective-permute-start(f32[256,256]{1,0:T(8,128)} %param.7), channel_id=1, source_target_pairs={{4,0},{5,1},{8,4},{9,5},{12,8},{13,9},{6,2},{7,3},{10,6},{11,7},{1... | collective-permute-start | bytes 786440 | tf_op jit(solution)/shard_map/ppermute | solution.py:17
  8.0 10.2 %collective-permute-start = (f32[256,256]{1,0:T(8,128)}, f32[256,256]{1,0:T(8,128)S(1)}, u32[]{:S(2)}, u32[]{:S(2)}) collective-permute-start(f32[256,256]{1,0:T(8,128)} %param.7), channel_id=1, source_target_pairs={{1,0},{4,1},{5,4},{8,5},{9,8},{12,9},{13,12},{3,2},{6,3},{7,6},{10... | collective-permute-start | bytes 786440 | tf_op jit(solution)/shard_map/ppermute | solution.py:17
  72.7 31.2 %collective-permute-start.3 = (bf16[64,8,2,256]{3,1,2,0:T(8,128)(2,1)}, bf16[64,8,2,256]{3,1,2,0:T(8,128)(2,1)S(1)}, u32[]{:S(2)}, u32[]{:S(2)}) collective-permute-start(bf16[64,8,2,256]{3,1,2,0:T(8,128)(2,1)} %copy.37), channel_id=1, source_target_pairs={{8,0},{12,4},{9,1},{13,5},{10,2},{14,6},{11,3},{15,7},{24,16},{28,... | collective-permute-start | bytes 1572872 | tf_op jit(solution)/shard_map/ppermute | solution.py:17
  74.0 54.1 %collective-permute-start.2 = (bf16[64,8,2,256]{3,1,2,0:T(8,128)(2,1)}, bf16[64,8,2,256]{3,1,2,0:T(8,128)(2,1)}, u32[]{:S(2)}, u32[]{:S(2)}) collective-permute-start(bf16[64,8,2,256]{3,1,2,0:T(8,128)(2,1)} %copy.37), channel_id=1, source_target_pairs={{4,0},{8,4},{12,8},{5,1},{9,5},{13,9},{6,2},{10,6},{14,10},{7,3},{... | collective-permute-start | bytes 1572872 | tf_op jit(solution)/shard_map/ppermute | solution.py:17
  128.1 1.3 copy-start
Sparse Core Ops, SparseCore 0:
  51.0 19.2 all-gather.3
where the time goes:
time: 171 us; the launch traced here: 170 us
  local copies, waits for them, and re-layouts  47.2 us (28%)
  matrix products  27.9 us (16%)
  blocking collectives  25.5 us (15%)
  other arithmetic  25 us (15%)
  waiting for transfers between devices  22.9 us (13%)
  between operations  15.6 us (9%)
  starting transfers between devices  5.46 us (3%)
    convert_element_type x3, local copies, waits for them, and re-layouts, transform(): term = cross_spectra(rows, partner, factor).astype(jnp.bfloat16)  35.9 us
    all_to_all x1, blocking collectives, body(): lax.all_to_all(lax.all_to_all(spectra, 'freq', split_axis=3, concat_axis=...  15.3 us
    dot_general x3, matrix products, transform(): jnp.einsum('pcf,fl->pcl', term, lag_table, preferred_element_type=jnp.flo...  15.2 us
    all_gather x1, waiting for transfers between devices, body(): full_block = lax.all_gather(block, 'freq', axis=3, tiled=True)  14.7 us
    convert_element_type x3, other arithmetic, transform(): term = cross_spectra(rows, partner, factor).astype(jnp.bfloat16)  13.9 us
    ppermute x4, waiting for transfers between devices, shifted(): lax.ppermute(value, axis, [(source, source + steps) for source in range(i...  8.16 us
    all_to_all x1, blocking collectives, body(): lax.all_to_all(spectra, 'freq', split_axis=3, concat_axis=0, tiled=True)  7.89 us
    broadcast_in_dim x1, other arithmetic, body(): return result[None]  6.38 us
  transfers between devices with their start and end apart: 5, of which 2 were waited for; matrix products, arithmetic and copies ran while one was open for 33% of the time, Pallas kernels for 0%

commit v1 on v0

v1 whole, which is shorter than its diff:
```python
import functools
import math

import jax
import jax.numpy as jnp
import numpy as np
from jax import lax
from jax.experimental import pallas as pl
from jax.experimental.pallas import tpu as pltpu
from jax.sharding import PartitionSpec as P

F = 256
REACH = 2
LAGS = 256
STEP = 256
LANES = 128
PACK = 16
EXTRA = 8
ROWS_PER_STEP = 16


def rotated(value, axis, steps):
    count = lax.axis_size(axis)
    return lax.ppermute(value, axis, [(source, (source + steps) % count) for source in range(count)])


def tables(span, windows):
    samples = np.arange(span)
    freqs = np.arange(F)
    angle = 2.0 * math.pi / span * (samples[:, None] * freqs[None, :] % span)
    basis = np.concatenate([np.cos(angle), -np.sin(angle)], axis=1) / math.sqrt(span)
    delays = np.arange(LAGS) - LAGS // 2
    angle = 2.0 * math.pi / span * (freqs[:, None] * delays[None, :] % span)
    lag = np.concatenate([np.cos(angle), -np.sin(angle)], axis=0) / math.sqrt(F)
    taper = 0.5 - 0.5 * np.cos(2.0 * math.pi / span * samples)
    return (
        jnp.asarray(basis.T.astype(np.float32), jnp.bfloat16),
        jnp.asarray((lag / windows).astype(np.float32), jnp.bfloat16),
        jnp.asarray(np.broadcast_to(taper[:, None], (span, LANES)), jnp.float32),
    )


def pack_kernel(dims, raw_ref, keep_ref, *send_refs):
    freq_count, blocks, chans, width, parts, tp = dims
    mine = lax.axis_index("freq")
    for shift, out in enumerate((keep_ref, *send_refs)):
        part = lax.rem(mine + shift, freq_count)
        for block in range(blocks):
            start = pl.multiple_of(block * chans + part * width, width)
            rows = raw_ref[pl.ds(start, width), :]
            stacked = jnp.concatenate([rows[:, i * tp : (i + 1) * tp] for i in range(parts)], axis=0)
            out[block] = stacked.T


def route_kernel(dims, offset_ref, *refs):
    pair_count, freq_count, blocks, tp, local = dims
    ins, rest = refs[:freq_count], refs[freq_count:]
    near, far, held = rest[:pair_count], rest[pair_count : 2 * pair_count], rest[-1]
    mine = lax.axis_index("freq")
    here = lax.axis_index("pair")
    for shift, source in enumerate(ins):
        owner = lax.rem(mine + freq_count - shift, freq_count)
        for block in range(blocks):
            held[owner * blocks + block] = source[block]
    lane = lax.broadcasted_iota(jnp.int32, (EXTRA, LANES), 1)
    note = jnp.zeros((EXTRA, LANES), jnp.float32)
    for i in range(local):
        note = jnp.where(lane == i, offset_ref[i].astype(jnp.float32), note)
    for shift in range(pair_count):
        near[shift][0:tp, :] = held[lax.rem(here + shift, pair_count)]
        near[shift][tp : tp + EXTRA, :] = note
        for ahead in range(1, REACH + 1):
            far[shift][ahead - 1] = held[lax.rem(here + shift + ahead, pair_count)]


def correlate_kernel(dims, mask_ref, *refs):
    (pair_count, freq_count, sub_count, local, seg, width, parts, tp, row_parts, windows, span) = dims
    near_count = freq_count * sub_count
    far_count = pair_count * sub_count
    near = refs[:near_count]
    far = refs[near_count : near_count + far_count]
    basis_ref, lag_ref, taper_ref, out_ref, starts, x_ref, spec_ref, row_ref, cross_ref = refs[
        near_count + far_count :
    ]
    total = windows * STEP
    cols = (REACH + 1) * width
    row_count = row_parts * width
    depth = 2 * windows * PACK
    wide = cross_ref.shape[2]
    step = pl.program_id(0)
    here = lax.axis_index("pair")
    mine = lax.axis_index("freq")
    core = lax.axis_index("sub")

    def place(slot, segment, piece):
        tile, lo = divmod(slot * width, LANES)
        for i in range(parts):
            base = pl.multiple_of(segment * seg + i * tp, tp)
            x_ref[tile, pl.ds(base, tp), lo : lo + width] = piece[:, i * width : (i + 1) * width]

    @pl.when(step == 0)
    def _():
        x_ref[:, total : total + span, :] = jnp.zeros((x_ref.shape[0], span, LANES), jnp.float32)
        if cols + row_count < x_ref.shape[0] * LANES:
            x_ref[x_ref.shape[0] - 1] = jnp.zeros(x_ref.shape[1:], jnp.float32)
        for turn in range(sub_count):
            source_core = lax.rem(core + sub_count - turn, sub_count)
            for shift in range(pair_count):
                source = lax.rem(here + pair_count - shift, pair_count)
                segment = source * sub_count + source_core
                piece = near[turn * freq_count]
                place(0, segment, piece[shift, 0:tp, :])
                note = piece[shift, tp : tp + EXTRA, :]
                for i in range(local):
                    number = jnp.max(note[:, i : i + 1]).astype(jnp.int32)
                    window = segment * local + i
                    starts[window] = window * STEP + number
                for ahead in range(REACH):
                    place(1 + ahead, segment, far[turn * pair_count + shift][ahead])
                for i in range(row_parts):
                    part = core * row_parts + i
                    for k in range(freq_count):

                        @pl.when(lax.rem(mine + freq_count - part, freq_count) == k)
                        def _(k=k, i=i, segment=segment, shift=shift, turn=turn):
                            place(REACH + 1 + i, segment, near[turn * freq_count + k][shift, 0:tp, :])

        def spectra(window, unused):
            tapered = []
            for tile in range(x_ref.shape[0]):
                values = x_ref[tile, pl.ds(starts[window], span), :]
                centred = values - jnp.mean(values, axis=0, keepdims=True)
                power = jnp.mean(centred * centred, axis=0, keepdims=True)
                tapered.append((centred * lax.rsqrt(power + 1e-05) * taper_ref[...]).astype(jnp.bfloat16))
            spec_ref[window] = jnp.dot(
                basis_ref[...], jnp.concatenate(tapered, axis=1), preferred_element_type=jnp.float32
            ).astype(jnp.bfloat16)
            return unused

        lax.fori_loop(0, windows, spectra, 0)
        lane = lax.broadcasted_iota(jnp.int32, (PACK, depth), 1)
        diagonal = lax.rem(lane, PACK) == lax.broadcasted_iota(jnp.int32, (PACK, depth), 0)
        lo = cols // LANES * LANES
        hi = -(-(cols + row_count) // LANES) * LANES

        def group(index, unused):
            real = pl.multiple_of(index * PACK, PACK)
            imag = pl.multiple_of(F + index * PACK, PACK)
            same, turned = [], []
            for window in range(windows):
                first = spec_ref[window, pl.ds(real, PACK), :]
                second = spec_ref[window, pl.ds(imag, PACK), :]
                same += [first, second]
                turned += [-second, first]
            same = jnp.concatenate(same, axis=0)
            turned = jnp.concatenate(turned, axis=0)
            right = jnp.concatenate([same[:, :wide], turned[:, :wide]], axis=1)
            row_ref[...] = same[:, lo:hi].astype(jnp.float32).T[cols - lo : cols - lo + row_count]
            left = jnp.concatenate(
                [
                    jnp.where(diagonal, jnp.broadcast_to(row_ref[r : r + 1, :], (PACK, depth)), 0.0).astype(
                        jnp.bfloat16
                    )
                    for r in range(row_count)
                ],
                axis=0,
            )
            term = jnp.dot(left, right, preferred_element_type=jnp.float32).astype(jnp.bfloat16)
            term = term.reshape(row_count, PACK, 2 * wide)
            cross_ref[:, pl.ds(real, PACK), :] = term[:, :, :wide]
            cross_ref[:, pl.ds(imag, PACK), :] = term[:, :, wide:]
            return unused

        lax.fori_loop(0, F // PACK, group, 0)

    keeps = [None] + [
        (here + ahead < pair_count) & (mask_ref[0, ahead - 1] == 1) for ahead in range(1, REACH + 1)
    ]
    for r in range(out_ref.shape[2]):
        result = lax.dot_general(
            cross_ref[step * out_ref.shape[2] + r],
            lag_ref[...],
            (((0,), (0,)), ((), ())),
            preferred_element_type=jnp.float32,
        )
        for ahead, keep in enumerate(keeps):
            value = result[ahead * width : (ahead + 1) * width]
            if keep is not None:
                value = jnp.where(keep, value, 0.0)
            out_ref[0, ahead, r] = value.astype(jnp.bfloat16)


def body(raw, offsets, pair_mask):
    pair_count = lax.axis_size("pair")
    freq_count = lax.axis_size("freq")
    sub_count = lax.axis_size("sub")
    local = offsets.shape[0]
    seg = raw.shape[1]
    span = 2 * F
    chans = raw.shape[0] * freq_count // pair_count
    blocks = pair_count // freq_count
    width = chans // freq_count
    row_count = chans // sub_count
    row_parts = row_count // width
    parts = LANES // width
    tp = seg // parts
    windows = pair_count * sub_count * local
    vmem = pl.BlockSpec(memory_space=pltpu.VMEM)
    smem = pl.BlockSpec(memory_space=pltpu.SMEM)
    unit = jax.ShapeDtypeStruct((blocks, tp, LANES), jnp.float32)
    packed = pl.pallas_call(
        functools.partial(pack_kernel, (freq_count, blocks, chans, width, parts, tp)),
        out_shape=[unit] * freq_count,
        in_specs=[vmem],
        out_specs=[vmem] * freq_count,
        name="pack",
    )(raw)
    shared = [packed[0]] + [rotated(packed[k], "freq", k) for k in range(1, freq_count)]
    routed = pl.pallas_call(
        functools.partial(route_kernel, (pair_count, freq_count, blocks, tp, local)),
        out_shape=[jax.ShapeDtypeStruct((tp + EXTRA, LANES), jnp.float32)] * pair_count
        + [jax.ShapeDtypeStruct((REACH, tp, LANES), jnp.float32)] * pair_count,
        in_specs=[smem] + [vmem] * freq_count,
        out_specs=[vmem] * (2 * pair_count),
        scratch_shapes=[pltpu.VMEM((pair_count, tp, LANES), jnp.float32)],
        name="route",
    )(offsets, *shared)
    near = jnp.stack(
        [routed[0]] + [rotated(routed[k], "pair", k) for k in range(1, pair_count)]
    )
    far = [routed[pair_count]] + [
        rotated(routed[pair_count + k], "pair", k) for k in range(1, pair_count)
    ]
    near = [near] + [rotated(near, "freq", k) for k in range(1, freq_count)]
    near_all = list(near)
    far_all = list(far)
    for turn in range(1, sub_count):
        near_all += [rotated(value, "sub", turn) for value in near]
        far_all += [rotated(value, "sub", turn) for value in far]
    basis, lag, taper = tables(span, windows)
    cols = (REACH + 1) * width
    tiles = -(-(cols + row_count) // LANES)
    wide = -(-cols // LANES) * LANES
    rows = math.gcd(ROWS_PER_STEP, row_count)
    dims = (pair_count, freq_count, sub_count, local, seg, width, parts, tp, row_parts, windows, span)
    return pl.pallas_call(
        functools.partial(correlate_kernel, dims),
        grid=(row_count // rows,),
        out_shape=jax.ShapeDtypeStruct((1, REACH + 1, row_count, width, LAGS), jnp.bfloat16),
        in_specs=[smem] + [vmem] * (len(near_all) + len(far_all) + 3),
        out_specs=pl.BlockSpec((1, REACH + 1, rows, width, LAGS), lambda i: (0, 0, i, 0, 0)),
        scratch_shapes=[
            pltpu.SMEM((windows,), jnp.int32),
            pltpu.VMEM((tiles, windows * STEP + span, LANES), jnp.float32),
            pltpu.VMEM((windows, span, tiles * LANES), jnp.bfloat16),
            pltpu.VMEM((row_count, 2 * windows * PACK), jnp.float32),
            pltpu.VMEM((row_count, span, wide), jnp.bfloat16),
        ],
        name="correlate",
    )(pair_mask, *near_all, *far_all, basis, lag, taper)


def solution(mesh):
    return jax.shard_map(
        body,
        mesh=mesh,
        in_specs=(P("freq", ("hour", "pair", "sub")), P(("hour", "pair", "sub")), P("pair", None)),
        out_specs=P(("hour", "pair"), None, "sub", "freq", None),
        check_vma=False,
    )
```

time: 171 us -> 64.8 us (0.38)
  local copies, waits for them, and re-layouts: 47.2 us -> 2.09 us
  matrix products: 27.9 us -> 0 us
  Pallas kernels: 0 us -> 26.2 us
  blocking collectives: 25.5 us -> 0 us
  other arithmetic: 25 us -> 0.91 us
  between operations: 15.6 us -> 0.75 us
  starting transfers between devices: 5.46 us -> 16.6 us
  waiting for transfers between devices: 22.9 us -> 17.9 us
    convert_element_type x3 -> x0, local copies, waits for them, and re-layouts: 35.9 us -> none  [transform(): term = cross_spectra(rows, partner, factor).astype(jnp.bfloat16)]
    dot_general x10 -> x0, matrix products: 27.9 us -> none  [the longest x3 15.2 us: transform(): jnp.einsum('pcf,fl->pcl', term, lag_table, preferred_element_type=jnp.flo...]
    pallas_call x0 -> x3, Pallas kernels: none -> 26.2 us  [the longest x1 22.5 us: body(): pl.pallas_call(functools.partial(correlate_kernel, dims), grid=(row_count...]
    all_to_all x2 -> x0, blocking collectives: 23.2 us -> none  [the longest x1 15.3 us: body(): lax.all_to_all(lax.all_to_all(spectra, 'freq', split_axis=3, concat_axis=...]
    convert_element_type x4 -> x0, other arithmetic: 16.5 us -> none  [the longest x3 13.9 us: transform(): term = cross_spectra(rows, partner, factor).astype(jnp.bfloat16)]
    all_gather x1 -> x0, waiting for transfers between devices: 14.7 us -> none  [body(): full_block = lax.all_gather(block, 'freq', axis=3, tiled=True)]
    ppermute x4 -> x14, starting transfers between devices: 5.46 us -> 16.6 us  [rotated(): lax.ppermute(value, axis, [(source, (source + steps) % count) for source...]
    ppermute x4 -> x14, waiting for transfers between devices: 8.16 us -> 17.9 us  [rotated(): lax.ppermute(value, axis, [(source, (source + steps) % count) for source...]
  transfers between devices with their start and end apart: 5 -> 14, of which waited for: 2 -> 9; matrix products, arithmetic and copies ran while one was open for 33% -> 0% of each run, Pallas kernels for 0% -> 0%
where the time goes in v1:
time: 64.8 us; the launch traced here: 64.3 us
  Pallas kernels  26.2 us (40%)
  waiting for transfers between devices  17.9 us (28%)
  starting transfers between devices  16.6 us (26%)
  local copies, waits for them, and re-layouts  2.09 us (3%)
  other arithmetic  0.91 us (1%)
  between operations  0.75 us (1%)
    pallas_call x1, Pallas kernels, body(): pl.pallas_call(functools.partial(correlate_kernel, dims), grid=(row_count...  22.5 us
    ppermute x14, waiting for transfers between devices, rotated(): lax.ppermute(value, axis, [(source, (source + steps) % count) for source...  17.9 us
    ppermute x14, starting transfers between devices, rotated(): lax.ppermute(value, axis, [(source, (source + steps) % count) for source...  16.6 us
    unnamed x24, local copies, waits for them, and re-layouts  2.09 us
    pallas_call x1, Pallas kernels, body(): pl.pallas_call(functools.partial(route_kernel, (pair_count, freq_count, b...  1.91 us
    pallas_call x1, Pallas kernels, body(): pl.pallas_call(functools.partial(pack_kernel, (freq_count, blocks, chans,...  1.74 us
  transfers between devices with their start and end apart: 14, of which 9 were waited for; matrix products, arithmetic and copies ran while one was open for 0% of the time, Pallas kernels for 0%

profile of v1, /device:TPU:0, one launch (start us, length us, event | category | flops | bytes accessed | tf_op | source)
XLA Modules:
  0.0 64.3 jit_solution(16198813109665468338)
XLA Ops:
  0.0 1.7 %pack.1 = (f32[2,128,128]{2,1,0:T(8,128)}, f32[2,128,128]{2,1,0:T(8,128)}) custom-call(f32[256,256]{1,0:T(8,128)} %raw_ref.1), custom_call_target="tpu_custom_call" | custom-call | tf_op jit(solution)/shard_map/pack/pallas_call | solution.py:211
  1.7 3.0 %collective-permute-start = (f32[2,128,128]{2,1,0:T(8,128)}, f32[2,128,128]{2,1,0:T(8,128)S(1)}, u32[]{:S(2)}, u32[]{:S(2)}) collective-permute-start(f32[2,128,128]{2,1,0:T(8,128)} %get-tuple-element.16), channel_id=1, source_target_pairs={{0,2},{2,0},{1,3},{3,1},{4,6},{6,4},{5,7},{7,5},{8,10},{10,8},{9,1... | collective-permute-start | bytes 393224 | tf_op jit(solution)/shard_map/ppermute | solution.py:24
  5.4 3.1 %collective-permute-done.refs_1_ = f32[2,128,128]{2,1,0:T(8,128)S(1)} collective-permute-done((f32[2,128,128]{2,1,0:T(8,128)}, f32[2,128,128]{2,1,0:T(8,128)S(1)}, u32[]{:S(2)}, u32[]{:S(2)}) %collective-permute-start) | collective-permute-done | bytes 131104 | tf_op jit(solution)/shard_map/ppermute | solution.py:24
  8.4 0.0 copy-start.11
  8.4 0.6 %copy-done.11 = f32[2,128,128]{2,1,0:T(8,128)} copy-done((f32[2,128,128]{2,1,0:T(8,128)}, f32[2,128,128]{2,1,0:T(8,128)S(1)}, u32[]{:S(2)}) %copy-start.11) | copy-done | bytes 131096
  9.1 1.9 %route.1 = (f32[136,128]{1,0:T(8,128)}, f32[136,128]{1,0:T(8,128)}, f32[136,128]{1,0:T(8,128)}, f32[136,128]{1,0:T(8,128)}, f32[2,128,128]{2,1,0:T(8,128)}, /*in...) custom-call(s32[1]{0:T(128)S(6)} %copy.7.offset_ref, ...), custom_call_target="tpu_custom_call" | custom-call | tf_op jit(solution)/shard_map/route/pallas_call | solution.py:219
  11.0 1.8 %collective-permute-start.1 = (f32[136,128]{1,0:T(8,128)}, f32[136,128]{1,0:T(8,128)S(1)}, u32[]{:S(2)}, u32[]{:S(2)}) collective-permute-start(f32[136,128]{1,0:T(8,128)} %get-tuple-element.18), channel_id=1, source_target_pairs={{0,4},{4,8},{8,12},{12,0},{1,5},{5,9},{9,13},{13,1},{2,6},{6,10},{... | collective-permute-start | bytes 208904 | tf_op jit(solution)/shard_map/ppermute | solution.py:24
  12.8 2.6 %collective-permute-start.2 = (f32[136,128]{1,0:T(8,128)}, f32[136,128]{1,0:T(8,128)S(1)}, u32[]{:S(2)}, u32[]{:S(2)}) collective-permute-start(f32[136,128]{1,0:T(8,128)} %get-tuple-element.19), channel_id=1, source_target_pairs={{0,8},{4,12},{8,0},{12,4},{1,9},{5,13},{9,1},{13,5},{2,10},{6,14},... | collective-permute-start | bytes 208904 | tf_op jit(solution)/shard_map/ppermute | solution.py:24
  15.4 1.4 %collective-permute-start.3 = (f32[136,128]{1,0:T(8,128)}, f32[136,128]{1,0:T(8,128)S(1)}, u32[]{:S(2)}, u32[]{:S(2)}) collective-permute-start(f32[136,128]{1,0:T(8,128)} %get-tuple-element.20), channel_id=1, source_target_pairs={{0,12},{4,0},{8,4},{12,8},{1,13},{5,1},{9,5},{13,9},{2,14},{6,2},{... | collective-permute-start | bytes 208904 | tf_op jit(solution)/shard_map/ppermute | solution.py:24
  16.7 1.4 %collective-permute-done.1 = f32[136,128]{1,0:T(8,128)S(1)} collective-permute-done((f32[136,128]{1,0:T(8,128)}, f32[136,128]{1,0:T(8,128)S(1)}, u32[]{:S(2)}, u32[]{:S(2)}) %collective-permute-start.1) | collective-permute-done | bytes 69664 | tf_op jit(solution)/shard_map/ppermute | solution.py:24
  18.1 1.9 %collective-permute-done.2 = f32[136,128]{1,0:T(8,128)S(1)} collective-permute-done((f32[136,128]{1,0:T(8,128)}, f32[136,128]{1,0:T(8,128)S(1)}, u32[]{:S(2)}, u32[]{:S(2)}) %collective-permute-start.2) | collective-permute-done | bytes 69664 | tf_op jit(solution)/shard_map/ppermute | solution.py:24
  20.1 0.3 collective-permute-done.3
  20.3 0.9 %pad_maximum_fusion.refs_0_ = f32[4,136,128]{2,1,0:T(8,128)S(1)} fusion(f32[1,136,128]{2,1,0:T(8,128)S(1)} %bitcast.7, f32[1,136,128]{2,1,0:T(8,128)S(1)} %bitcast.6, f32[1,136,128]{2,1,0:T(8,128)S(1)} %bitcast.5, f32[1,136,128]{2,1,0:T(8,128)} %bitcast.4), kind=kLoop, calls=%fused_computation | loop fusion | flops 208896 | bytes 557056 | tf_op jit(solution)/shard_map/stack | solution.py:228
  21.2 0.0 copy-start
  21.2 1.6 %collective-permute-start.4 = (f32[4,136,128]{2,1,0:T(8,128)S(1)}, f32[4,136,128]{2,1,0:T(8,128)S(1)}, u32[]{:S(2)}, u32[]{:S(2)}) collective-permute-start(f32[4,136,128]{2,1,0:T(8,128)S(1)} %pad_maximum_fusion.refs_0_), channel_id=1, source_target_pairs={{0,2},{2,0},{1,3},{3,1},{4,6},{6,4},{5,7},{7,5},{8,10},{10,8},{9,1... | collective-permute-start | bytes 835592 | tf_op jit(solution)/shard_map/ppermute | solution.py:24
  22.8 1.0 %collective-permute-start.7 = (f32[2,128,128]{2,1,0:T(8,128)}, f32[2,128,128]{2,1,0:T(8,128)S(1)}, u32[]{:S(2)}, u32[]{:S(2)}) collective-permute-start(f32[2,128,128]{2,1,0:T(8,128)} %get-tuple-element.22), channel_id=1, source_target_pairs={{0,4},{4,8},{8,12},{12,0},{1,5},{5,9},{9,13},{13,1},{2,6},{6,10},{... | collective-permute-start | bytes 393224 | tf_op jit(solution)/shard_map/ppermute | solution.py:24
  23.9 0.0 collective-permute-start.5
  23.9 4.3 %collective-permute-done.4.refs_1_ = f32[4,136,128]{2,1,0:T(8,128)S(1)} collective-permute-done((f32[4,136,128]{2,1,0:T(8,128)S(1)}, f32[4,136,128]{2,1,0:T(8,128)S(1)}, u32[]{:S(2)}, u32[]{:S(2)}) %collective-permute-start.4) | collective-permute-done | bytes 278560 | tf_op jit(solution)/shard_map/ppermute | solution.py:24
  28.1 0.0 copy-start.1
  28.1 0.0 collective-permute-start.6
  28.1 1.3 %collective-permute-start.8 = (f32[2,128,128]{2,1,0:T(8,128)}, f32[2,128,128]{2,1,0:T(8,128)S(1)}, u32[]{:S(2)}, u32[]{:S(2)}) collective-permute-start(f32[2,128,128]{2,1,0:T(8,128)} %get-tuple-element.23), channel_id=1, source_target_pairs={{0,8},{4,12},{8,0},{12,4},{1,9},{5,13},{9,1},{13,5},{2,10},{6,14},... | collective-permute-start | bytes 393224 | tf_op jit(solution)/shard_map/ppermute | solution.py:24
  29.5 3.3 %collective-permute-start.9 = (f32[2,128,128]{2,1,0:T(8,128)}, f32[2,128,128]{2,1,0:T(8,128)S(1)}, u32[]{:S(2)}, u32[]{:S(2)}) collective-permute-start(f32[2,128,128]{2,1,0:T(8,128)} %get-tuple-element.24), channel_id=1, source_target_pairs={{0,12},{4,0},{8,4},{12,8},{1,13},{5,1},{9,5},{13,9},{2,14},{6,2},{... | collective-permute-start | bytes 393224 | tf_op jit(solution)/shard_map/ppermute | solution.py:24
  32.7 0.0 collective-permute-done.7.refs_5_
  32.7 0.0 copy-start.4
  32.7 0.0 collective-permute-start.10
  32.7 5.7 %collective-permute-done.8.refs_6_ = f32[2,128,128]{2,1,0:T(8,128)S(1)} collective-permute-done((f32[2,128,128]{2,1,0:T(8,128)}, f32[2,128,128]{2,1,0:T(8,128)S(1)}, u32[]{:S(2)}, u32[]{:S(2)}) %collective-permute-start.8) | collective-permute-done | bytes 131104 | tf_op jit(solution)/shard_map/ppermute | solution.py:24
  38.4 0.0 copy-start.5
  38.4 0.0 collective-permute-start.11
  38.4 0.0 collective-permute-done.9.refs_7_
  38.5 0.0 copy-start.6
  38.5 0.5 collective-permute-start.12
  39.0 0.0 collective-permute-done.10.refs_8_
  39.0 0.0 copy-start.7
  39.0 0.1 collective-permute-start.13
  39.1 0.7 %collective-permute-done.11.refs_9_ = f32[2,128,128]{2,1,0:T(8,128)S(1)} collective-permute-done((f32[2,128,128]{2,1,0:T(8,128)S(1)}, f32[2,128,128]{2,1,0:T(8,128)S(1)}, u32[]{:S(2)}, u32[]{:S(2)}) %collective-permute-start.11) | collective-permute-done | bytes 131104 | tf_op jit(solution)/shard_map/ppermute | solution.py:24
  39.8 0.0 copy-start.8
  39.8 0.2 collective-permute-done.12.refs_10_
  40.0 0.0 copy-start.9
  40.0 0.3 collective-permute-done.13.refs_11_
  40.3 0.0 copy-start.10
  40.3 0.0 collective-permute-done.5.refs_2_
  40.3 0.0 copy-start.2
  40.3 0.0 collective-permute-done.6.refs_3_
  40.3 0.0 copy-done
  40.3 0.0 copy-done.1
  40.3 0.0 copy-done.4
  40.4 0.0 copy-done.5
  40.4 0.0 copy-done.6
  40.4 0.0 copy-done.7
  40.4 0.0 copy-done.8
  40.4 0.2 copy-done.9
  40.6 0.3 copy-done.10
  41.0 0.1 copy-done.2
  41.1 0.0 copy-start.3
  41.1 0.7 %copy-done.3 = f32[4,136,128]{2,1,0:T(8,128)} copy-done((f32[4,136,128]{2,1,0:T(8,128)}, f32[4,136,128]{2,1,0:T(8,128)S(1)}, u32[]{:S(2)}) %copy-start.3) | copy-done | bytes 278552
  41.8 22.5 %correlate.1 = bf16[1,3,64,64,256]{4,3,2,1,0:T(8,128)(2,1)} custom-call(s32[1,2]{1,0:T(1,128)} %mask_ref.1, f32[4,136,128]{2,1,0:T(8,128)} %copy-done, f32[4,136,128]{2,1,0:T(8,128)} %copy-done.1, f32[4,136,128]{2,1,0:T(8,128)} %copy-done.2, f32[4,136,128]{2,1,0:T(8,128)} %copy-done.3, f32[2,128,128]{2,1,0:T(8,128)} %get-tuple-element.21.refs_4_, ...), custom_call_target="tpu_custom_call" | custom-call | tf_op jit(solution)/shard_map/correlate/pallas_call | solution.py:246
Async XLA Ops:
  1.7 6.7 %collective-permute-start = (f32[2,128,128]{2,1,0:T(8,128)}, f32[2,128,128]{2,1,0:T(8,128)S(1)}, u32[]{:S(2)}, u32[]{:S(2)}) collective-permute-start(f32[2,128,128]{2,1,0:T(8,128)} %get-tuple-element.16), channel_id=1, source_target_pairs={{0,2},{2,0},{1,3},{3,1},{4,6},{6,4},{5,7},{7,5},{8,10},{10,8},{9,1... | collective-permute-start | bytes 393224 | tf_op jit(solution)/shard_map/ppermute | solution.py:24
  8.4 0.7 %copy-start.11 = (f32[2,128,128]{2,1,0:T(8,128)}, f32[2,128,128]{2,1,0:T(8,128)S(1)}, u32[]{:S(2)}) copy-start(f32[2,128,128]{2,1,0:T(8,128)S(1)} %collective-permute-done.refs_1_) | copy-start | bytes 393220
  11.0 7.1 %collective-permute-start.1 = (f32[136,128]{1,0:T(8,128)}, f32[136,128]{1,0:T(8,128)S(1)}, u32[]{:S(2)}, u32[]{:S(2)}) collective-permute-start(f32[136,128]{1,0:T(8,128)} %get-tuple-element.18), channel_id=1, source_target_pairs={{0,4},{4,8},{8,12},{12,0},{1,5},{5,9},{9,13},{13,1},{2,6},{6,10},{... | collective-permute-start | bytes 208904 | tf_op jit(solution)/shard_map/ppermute | solution.py:24
  12.8 7.2 %collective-permute-start.2 = (f32[136,128]{1,0:T(8,128)}, f32[136,128]{1,0:T(8,128)S(1)}, u32[]{:S(2)}, u32[]{:S(2)}) collective-permute-start(f32[136,128]{1,0:T(8,128)} %get-tuple-element.19), channel_id=1, source_target_pairs={{0,8},{4,12},{8,0},{12,4},{1,9},{5,13},{9,1},{13,5},{2,10},{6,14},... | collective-permute-start | bytes 208904 | tf_op jit(solution)/shard_map/ppermute | solution.py:24
  15.4 4.9 %collective-permute-start.3 = (f32[136,128]{1,0:T(8,128)}, f32[136,128]{1,0:T(8,128)S(1)}, u32[]{:S(2)}, u32[]{:S(2)}) collective-permute-start(f32[136,128]{1,0:T(8,128)} %get-tuple-element.20), channel_id=1, source_target_pairs={{0,12},{4,0},{8,4},{12,8},{1,13},{5,1},{9,5},{13,9},{2,14},{6,2},{... | collective-permute-start | bytes 208904 | tf_op jit(solution)/shard_map/ppermute | solution.py:24
  21.2 19.1 %copy-start = (f32[4,136,128]{2,1,0:T(8,128)}, f32[4,136,128]{2,1,0:T(8,128)S(1)}, u32[]{:S(2)}) copy-start(f32[4,136,128]{2,1,0:T(8,128)S(1)} %pad_maximum_fusion.refs_0_) | copy-start | bytes 835588
  21.2 6.9 %collective-permute-start.4 = (f32[4,136,128]{2,1,0:T(8,128)S(1)}, f32[4,136,128]{2,1,0:T(8,128)S(1)}, u32[]{:S(2)}, u32[]{:S(2)}) collective-permute-start(f32[4,136,128]{2,1,0:T(8,128)S(1)} %pad_maximum_fusion.refs_0_), channel_id=1, source_target_pairs={{0,2},{2,0},{1,3},{3,1},{4,6},{6,4},{5,7},{7,5},{8,10},{10,8},{9,1... | collective-permute-start | bytes 835592 | tf_op jit(solution)/shard_map/ppermute | solution.py:24
  22.8 9.9 %collective-permute-start.7 = (f32[2,128,128]{2,1,0:T(8,128)}, f32[2,128,128]{2,1,0:T(8,128)S(1)}, u32[]{:S(2)}, u32[]{:S(2)}) collective-permute-start(f32[2,128,128]{2,1,0:T(8,128)} %get-tuple-element.22), channel_id=1, source_target_pairs={{0,4},{4,8},{8,12},{12,0},{1,5},{5,9},{9,13},{13,1},{2,6},{6,10},{... | collective-permute-start | bytes 393224 | tf_op jit(solution)/shard_map/ppermute | solution.py:24
  23.9 16.4 %collective-permute-start.5 = (f32[4,136,128]{2,1,0:T(8,128)S(1)}, f32[4,136,128]{2,1,0:T(8,128)S(1)}, u32[]{:S(2)}, u32[]{:S(2)}) collective-permute-start(f32[4,136,128]{2,1,0:T(8,128)S(1)} %pad_maximum_fusion.refs_0_), channel_id=1, source_target_pairs={{0,1},{1,0},{2,3},{3,2},{4,5},{5,4},{6,7},{7,6},{8,9},{9,8},{10,11... | collective-permute-start | bytes 835592 | tf_op jit(solution)/shard_map/ppermute | solution.py:24
  28.1 12.2 %copy-start.1 = (f32[4,136,128]{2,1,0:T(8,128)}, f32[4,136,128]{2,1,0:T(8,128)S(1)}, u32[]{:S(2)}) copy-start(f32[4,136,128]{2,1,0:T(8,128)S(1)} %collective-permute-done.4.refs_1_) | copy-start | bytes 835588
  28.1 12.2 %collective-permute-start.6 = (f32[4,136,128]{2,1,0:T(8,128)S(1)}, f32[4,136,128]{2,1,0:T(8,128)S(1)}, u32[]{:S(2)}, u32[]{:S(2)}) collective-permute-start(f32[4,136,128]{2,1,0:T(8,128)S(1)} %collective-permute-done.4.refs_1_), channel_id=1, source_target_pairs={{0,1},{1,0},{2,3},{3,2},{4,5},{5,4},{6,7},{7,6},{8,9},{9,8},{10,11... | collective-permute-start | bytes 835592 | tf_op jit(solution)/shard_map/ppermute | solution.py:24
  28.1 10.3 %collective-permute-start.8 = (f32[2,128,128]{2,1,0:T(8,128)}, f32[2,128,128]{2,1,0:T(8,128)S(1)}, u32[]{:S(2)}, u32[]{:S(2)}) collective-permute-start(f32[2,128,128]{2,1,0:T(8,128)} %get-tuple-element.23), channel_id=1, source_target_pairs={{0,8},{4,12},{8,0},{12,4},{1,9},{5,13},{9,1},{13,5},{2,10},{6,14},... | collective-permute-start | bytes 393224 | tf_op jit(solution)/shard_map/ppermute | solution.py:24
  29.5 9.0 %collective-permute-start.9 = (f32[2,128,128]{2,1,0:T(8,128)}, f32[2,128,128]{2,1,0:T(8,128)S(1)}, u32[]{:S(2)}, u32[]{:S(2)}) collective-permute-start(f32[2,128,128]{2,1,0:T(8,128)} %get-tuple-element.24), channel_id=1, source_target_pairs={{0,12},{4,0},{8,4},{12,8},{1,13},{5,1},{9,5},{13,9},{2,14},{6,2},{... | collective-permute-start | bytes 393224 | tf_op jit(solution)/shard_map/ppermute | solution.py:24
  32.7 7.6 %copy-start.4 = (f32[2,128,128]{2,1,0:T(8,128)}, f32[2,128,128]{2,1,0:T(8,128)S(1)}, u32[]{:S(2)}) copy-start(f32[2,128,128]{2,1,0:T(8,128)S(1)} %collective-permute-done.7.refs_5_) | copy-start | bytes 393220
  32.7 6.2 %collective-permute-start.10 = (f32[2,128,128]{2,1,0:T(8,128)}, f32[2,128,128]{2,1,0:T(8,128)S(1)}, u32[]{:S(2)}, u32[]{:S(2)}) collective-permute-start(f32[2,128,128]{2,1,0:T(8,128)} %get-tuple-element.21.refs_4_), channel_id=1, source_target_pairs={{0,1},{1,0},{2,3},{3,2},{4,5},{5,4},{6,7},{7,6},{8,9},{9,8},{10,11... | collective-permute-start | bytes 393224 | tf_op jit(solution)/shard_map/ppermute | solution.py:24
  38.4 1.9 %copy-start.5 = (f32[2,128,128]{2,1,0:T(8,128)}, f32[2,128,128]{2,1,0:T(8,128)S(1)}, u32[]{:S(2)}) copy-start(f32[2,128,128]{2,1,0:T(8,128)S(1)} %collective-permute-done.8.refs_6_) | copy-start | bytes 393220
  38.4 1.3 %collective-permute-start.11 = (f32[2,128,128]{2,1,0:T(8,128)S(1)}, f32[2,128,128]{2,1,0:T(8,128)S(1)}, u32[]{:S(2)}, u32[]{:S(2)}) collective-permute-start(f32[2,128,128]{2,1,0:T(8,128)S(1)} %collective-permute-done.7.refs_5_), channel_id=1, source_target_pairs={{0,1},{1,0},{2,3},{3,2},{4,5},{5,4},{6,7},{7,6},{8,9},{9,8},{10,11... | collective-permute-start | bytes 393224 | tf_op jit(solution)/shard_map/ppermute | solution.py:24
  38.5 1.9 %copy-start.6 = (f32[2,128,128]{2,1,0:T(8,128)}, f32[2,128,128]{2,1,0:T(8,128)S(1)}, u32[]{:S(2)}) copy-start(f32[2,128,128]{2,1,0:T(8,128)S(1)} %collective-permute-done.9.refs_7_) | copy-start | bytes 393220
  38.5 1.5 %collective-permute-start.12 = (f32[2,128,128]{2,1,0:T(8,128)S(1)}, f32[2,128,128]{2,1,0:T(8,128)S(1)}, u32[]{:S(2)}, u32[]{:S(2)}) collective-permute-start(f32[2,128,128]{2,1,0:T(8,128)S(1)} %collective-permute-done.8.refs_6_), channel_id=1, source_target_pairs={{0,1},{1,0},{2,3},{3,2},{4,5},{5,4},{6,7},{7,6},{8,9},{9,8},{10,11... | collective-permute-start | bytes 393224 | tf_op jit(solution)/shard_map/ppermute | solution.py:24
  39.0 1.4 %copy-start.7 = (f32[2,128,128]{2,1,0:T(8,128)}, f32[2,128,128]{2,1,0:T(8,128)S(1)}, u32[]{:S(2)}) copy-start(f32[2,128,128]{2,1,0:T(8,128)S(1)} %collective-permute-done.10.refs_8_) | copy-start | bytes 393220
  39.0 1.3 %collective-permute-start.13 = (f32[2,128,128]{2,1,0:T(8,128)S(1)}, f32[2,128,128]{2,1,0:T(8,128)S(1)}, u32[]{:S(2)}, u32[]{:S(2)}) collective-permute-start(f32[2,128,128]{2,1,0:T(8,128)S(1)} %collective-permute-done.9.refs_7_), channel_id=1, source_target_pairs={{0,1},{1,0},{2,3},{3,2},{4,5},{5,4},{6,7},{7,6},{8,9},{9,8},{10,11... | collective-permute-start | bytes 393224 | tf_op jit(solution)/shard_map/ppermute | solution.py:24
  39.8 0.6 %copy-start.8 = (f32[2,128,128]{2,1,0:T(8,128)}, f32[2,128,128]{2,1,0:T(8,128)S(1)}, u32[]{:S(2)}) copy-start(f32[2,128,128]{2,1,0:T(8,128)S(1)} %collective-permute-done.11.refs_9_) | copy-start | bytes 393220
  40.0 0.6 copy-start.9
  40.3 0.7 %copy-start.10 = (f32[2,128,128]{2,1,0:T(8,128)}, f32[2,128,128]{2,1,0:T(8,128)S(1)}, u32[]{:S(2)}) copy-start(f32[2,128,128]{2,1,0:T(8,128)S(1)} %collective-permute-done.13.refs_11_) | copy-start | bytes 393220
  40.3 0.8 %copy-start.2 = (f32[4,136,128]{2,1,0:T(8,128)}, f32[4,136,128]{2,1,0:T(8,128)S(1)}, u32[]{:S(2)}) copy-start(f32[4,136,128]{2,1,0:T(8,128)S(1)} %collective-permute-done.5.refs_2_) | copy-start | bytes 835588
  41.1 0.7 %copy-start.3 = (f32[4,136,128]{2,1,0:T(8,128)}, f32[4,136,128]{2,1,0:T(8,128)S(1)}, u32[]{:S(2)}) copy-start(f32[4,136,128]{2,1,0:T(8,128)S(1)} %collective-permute-done.6.refs_3_) | copy-start | bytes 835588
